TPU v7x, 256 devices: a whole 4x4x8 slice. The times are simulated.
256 devices in a mesh: head: 8 (over z_lo, core), blk: 32 (over y, x, z_hi).
Axes of the slice: x: 4, y: 4, z: 8 (z_hi: 2, z_lo: 4; z = z_hi * 4 + z_lo), core: 2. Of those that a mesh axis runs over, the one named last changes fastest.
Arguments:
- query_act: bfloat16 [8192, 5120], P(('blk', 'head')), may hold values from -6 to 6
- key_act: bfloat16 [8192, 1024], P(('blk', 'head')), may hold values from -6 to 6
- value_act: bfloat16 [8192, 1024], P(('blk', 'head')), may hold values from -6 to 6
- attn_out: bfloat16 [8192, 5120], P(('blk', 'head')), may hold values from -4 to 4
- grad_out: bfloat16 [8192, 5120], P(('blk', 'head')), may hold values from -6 to 6
- log_sum: float32 [8192, 40], P(('blk', 'head')), may hold values from 5 to 6.5
- kv_lists: int32 [64, 32], P('blk'), may hold values from -1 to 63, as said below
Outputs:
- grad_query: bfloat16 [8192, 5120], P(('blk', 'head'))
- grad_key: bfloat16 [8192, 1024], P(('blk', 'head'))
- grad_value: bfloat16 [8192, 1024], P(('blk', 'head'))
Inputs may be any that keep to these rules, and one draw needn't show every extreme that they name: `kv_lists`: the pack is made of prompt trees: the first holds 16 blocks, the last 16, and those between 32 blocks each, in order. A tree is a prompt, then branches. Row r names in rising order the blocks whose keys block r sees (the tree's prompt blocks up to r, and the earlier blocks of r's branch), then -1 to the end. Every entry lies in the same tree as r and is at most r; r itself is always named.
All inputs are finite; a program needn't handle non-finite values.
Results may differ from a plain program's by a relative error of at most 0.0049.
Values may be sent and summed in bfloat16 or wider, within the bound.
A program may use at most 64 MiB of HBM per device.

v0:
```python
import jax
import jax.numpy as jnp
from jax import lax
from jax.sharding import PartitionSpec as P

QH = 40
KVH = 8
HD = 128
BLOCK = 128


def passed_along(array, axis, by):
    size = lax.axis_size(axis)
    pairs = [(i, i + by) for i in range(size) if 0 <= i + by < size]
    return lax.ppermute(array, axis, pairs)


def shifted(array, axis, by):
    size = lax.axis_size(axis)
    return lax.ppermute(array, axis, [(i, (i + by) % size) for i in range(size)])


def head_delta(grad_rows, out_rows, heads):
    count = grad_rows.shape[0]
    return jnp.einsum(
        "thd,thd->th",
        grad_rows.reshape(count, heads, HD),
        out_rows.reshape(count, heads, HD),
        preferred_element_type=jnp.float32,
    )


def local(query_act, key_act, value_act, attn_out, grad_out, log_sum, kv_lists):
    head_count = lax.axis_size("head")
    blk_count = lax.axis_size("blk")
    query_rows, key_rows, value_rows, grad_rows, total_rows, out_rows = (
        lax.all_to_all(
            query_act.astype(jnp.float32), "head", split_axis=1, concat_axis=0, tiled=True
        ).astype(query_act.dtype),
        lax.all_to_all(
            key_act.astype(jnp.float32), "head", split_axis=1, concat_axis=0, tiled=True
        ).astype(key_act.dtype),
        lax.all_to_all(
            value_act.astype(jnp.float32), "head", split_axis=1, concat_axis=0, tiled=True
        ).astype(value_act.dtype),
        lax.all_to_all(
            grad_out.astype(jnp.float32), "head", split_axis=1, concat_axis=0, tiled=True
        ).astype(grad_out.dtype),
        lax.all_to_all(log_sum, "head", split_axis=1, concat_axis=0, tiled=True),
        lax.all_to_all(
            attn_out.astype(jnp.float32), "head", split_axis=1, concat_axis=0, tiled=True
        ).astype(attn_out.dtype),
    )
    delta_rows = head_delta(grad_rows, out_rows, QH // head_count)
    tokens = query_rows.shape[0]
    local_heads = KVH // head_count
    group_size = QH // KVH
    blocks_dev = tokens // BLOCK
    scaling = HD ** (-0.5)
    queries = query_rows.reshape(tokens, local_heads, group_size, HD)
    out_grads = grad_rows.reshape(tokens, local_heads, group_size, HD)
    row_totals = total_rows.reshape(tokens, local_heads, group_size).transpose(1, 2, 0)[
        :, :, :, None
    ]
    row_deltas = delta_rows.reshape(tokens, local_heads, group_size).transpose(1, 2, 0)[
        :, :, :, None
    ]
    position = lax.axis_index("blk")
    query_pos = position * tokens + jnp.arange(tokens, dtype=jnp.int32)

    def block_mask(rotation):
        source = (position - rotation) % blk_count
        key_ids = source * blocks_dev + jnp.arange(blocks_dev, dtype=jnp.int32)
        listed = jnp.any(kv_lists[:, :, None] == key_ids[None, None, :], axis=1)
        key_pos = source * tokens + jnp.arange(tokens, dtype=jnp.int32)
        return (listed, key_pos)

    def attend(kv_pair, key_sums, query_grad, listed, key_pos):
        visible = jnp.repeat(jnp.repeat(listed, BLOCK, axis=0), BLOCK, axis=1) & (
            key_pos[None, :] <= query_pos[:, None]
        )
        key_block = kv_pair[0].reshape(tokens, local_heads, HD)
        value_block = kv_pair[1].reshape(tokens, local_heads, HD)
        scores = (
            jnp.einsum("tkgd,skd->kgts", queries, key_block, preferred_element_type=jnp.float32)
            * scaling
        )
        weights = jnp.where(visible, jnp.exp(scores - row_totals), 0.0)
        grad_probs = jnp.einsum(
            "tkgd,skd->kgts", out_grads, value_block, preferred_element_type=jnp.float32
        )
        grad_scores = (weights * (grad_probs - row_deltas)).astype(jnp.bfloat16)
        probs_low = weights.astype(jnp.bfloat16)
        value_part = jnp.einsum(
            "kgts,tkgd->skd", probs_low, out_grads, preferred_element_type=jnp.float32
        )
        key_part = (
            jnp.einsum("kgts,tkgd->skd", grad_scores, queries, preferred_element_type=jnp.float32)
            * scaling
        )
        query_part = (
            jnp.einsum("kgts,skd->tkgd", grad_scores, key_block, preferred_element_type=jnp.float32)
            * scaling
        )
        added = jnp.stack(
            [
                key_part.reshape(tokens, local_heads * HD),
                value_part.reshape(tokens, local_heads * HD),
            ]
        )
        return (key_sums + added, query_grad + query_part)

    def visit(rotation, kv_pair, key_sums, query_grad):
        listed, key_pos = block_mask(rotation)
        return attend(kv_pair, key_sums, query_grad, listed, key_pos)

    kv_pair = jnp.stack([key_rows, value_rows])
    empty_sums = jnp.zeros((2, tokens, local_heads * HD), jnp.float32)
    empty_grad = jnp.zeros((tokens, local_heads, group_size, HD), jnp.float32)

    def advance(rotation, carried):
        kv_here, key_sums, query_grad = carried
        arrived = passed_along(kv_here, "blk", 1)
        key_sums, query_grad = visit(rotation, kv_here, key_sums, query_grad)
        key_sums = shifted(key_sums, "blk", 1)
        return (arrived, key_sums, query_grad)

    kv_here, key_sums, query_grad = lax.fori_loop(
        0, blk_count - 1, advance, (kv_pair, empty_sums, empty_grad)
    )
    key_sums, query_grad = visit(blk_count - 1, kv_here, key_sums, query_grad)
    key_sums = shifted(key_sums.astype(jnp.bfloat16), "blk", 1 - blk_count).astype(key_sums.dtype)
    query_low = query_grad.reshape(tokens, local_heads * group_size * HD).astype(jnp.bfloat16)
    key_low = key_sums[0].astype(jnp.bfloat16)
    value_low = key_sums[1].astype(jnp.bfloat16)
    grad_query, grad_key, grad_value = (
        lax.all_to_all(query_low, "head", split_axis=0, concat_axis=1, tiled=True),
        lax.all_to_all(key_low, "head", split_axis=0, concat_axis=1, tiled=True),
        lax.all_to_all(value_low, "head", split_axis=0, concat_axis=1, tiled=True),
    )
    return (grad_query, grad_key, grad_value)


def solution(mesh):
    return jax.shard_map(
        local,
        mesh=mesh,
        in_specs=(
            P(("blk", "head"), None),
            P(("blk", "head"), None),
            P(("blk", "head"), None),
            P(("blk", "head"), None),
            P(("blk", "head"), None),
            P(("blk", "head"), None),
            P("blk", None),
        ),
        out_specs=(P(("blk", "head"), None), P(("blk", "head"), None), P(("blk", "head"), None)),
        check_vma=False,
    )
```

profile of v0, /device:TPU:9, one launch (start us, length us, event | category | flops | bytes accessed | tf_op | source)
XLA Modules:
  0.0 878.3 jit_solution(12147705580826864450)
XLA Ops:
  2.2 6.6 all-to-all-start.3
  37.0 9.3 %all-to-all-done.2 = bf16[32,8,640]{2,0,1:T(8,128)(2,1)S(1)} async-done(((bf16[32,8,640]{2,0,1:T(8,128)(2,1)}), bf16[32,8,640]{2,0,1:T(8,128)(2,1)S(1)}, u32[]{:S(2)}, u32[]{:S(2)}) %all-to-all-start.2) | async-done | bytes 327712 | tf_op jit(solution)/shard_map/all_to_all | solution.py:37
  51.8 9.0 %all-to-all-done.4 = bf16[32,8,640]{2,0,1:T(8,128)(2,1)S(1)} async-done(((bf16[32,8,640]{2,0,1:T(8,128)(2,1)}), bf16[32,8,640]{2,0,1:T(8,128)(2,1)S(1)}, u32[]{:S(2)}, u32[]{:S(2)}) %all-to-all-start.4) | async-done | bytes 327712 | tf_op jit(solution)/shard_map/all_to_all | solution.py:46
  60.8 5.1 all-to-all-start.5
  69.7 6.3 all-to-all-done.5
  77.8 697.4 %while.20 = (s32[]{:T(128)}, bf16[2,256,128]{2,1,0:T(8,128)(2,1)S(1)}, f32[2,256,128]{2,1,0:T(8,128)S(1)}, f32[256,1,5,128]{3,0,2,1:T(8,128)S(1)}, s32[2,32]{1,0...) while((s32[]{:T(128)}, ...), condition=%wide.region_2.3_spmd.clone, body=%wide.region_0.2_spmd.clone.sunk | while | flops 422511360 | bytes 11754164 | solution.py:128
  77.8 6.2 collective-permute-start
  88.7 6.9 collective-permute-done
  95.6 5.8 collective-permute-done.1
  114.6 7.8 collective-permute-done.1
  126.4 5.5 collective-permute-start.1
  135.1 5.7 collective-permute-done.1
  151.2 6.3 collective-permute-done
  160.5 5.0 collective-permute-start
  167.6 7.1 collective-permute-start.1
  189.5 9.2 %collective-permute-done = bf16[2,256,128]{2,1,0:T(8,128)(2,1)S(1)} collective-permute-done((bf16[2,256,128]{2,1,0:T(8,128)(2,1)S(1)}, bf16[2,256,128]{2,1,0:T(8,128)(2,1)S(1)}, u32[]{:S(2)}, u32[]{:S(2)}) %collective-permute-start) | collective-permute-done | bytes 131104 | tf_op jit(solution)/shard_map/while/body/eval_jaxpr/ppermute | solution.py:15
  211.1 10.0 %collective-permute-done = bf16[2,256,128]{2,1,0:T(8,128)(2,1)S(1)} collective-permute-done((bf16[2,256,128]{2,1,0:T(8,128)(2,1)S(1)}, bf16[2,256,128]{2,1,0:T(8,128)(2,1)S(1)}, u32[]{:S(2)}, u32[]{:S(2)}) %collective-permute-start) | collective-permute-done | bytes 131104 | tf_op jit(solution)/shard_map/while/body/eval_jaxpr/ppermute | solution.py:15
  233.8 9.0 %collective-permute-done = bf16[2,256,128]{2,1,0:T(8,128)(2,1)S(1)} collective-permute-done((bf16[2,256,128]{2,1,0:T(8,128)(2,1)S(1)}, bf16[2,256,128]{2,1,0:T(8,128)(2,1)S(1)}, u32[]{:S(2)}, u32[]{:S(2)}) %collective-permute-start) | collective-permute-done | bytes 131104 | tf_op jit(solution)/shard_map/while/body/eval_jaxpr/ppermute | solution.py:15
  253.7 12.0 %collective-permute-done = bf16[2,256,128]{2,1,0:T(8,128)(2,1)S(1)} collective-permute-done((bf16[2,256,128]{2,1,0:T(8,128)(2,1)S(1)}, bf16[2,256,128]{2,1,0:T(8,128)(2,1)S(1)}, u32[]{:S(2)}, u32[]{:S(2)}) %collective-permute-start) | collective-permute-done | bytes 131104 | tf_op jit(solution)/shard_map/while/body/eval_jaxpr/ppermute | solution.py:15
  265.7 5.6 collective-permute-done.1
  271.3 8.9 %collective-permute-start = (bf16[2,256,128]{2,1,0:T(8,128)(2,1)S(1)}, bf16[2,256,128]{2,1,0:T(8,128)(2,1)S(1)}, u32[]{:S(2)}, u32[]{:S(2)}) collective-permute-start(bf16[2,256,128]{2,1,0:T(8,128)(2,1)S(1)} %copy.135), channel_id=1, source_target_pairs={{0,1},{1,2},{2,3},{3,4},{4,5},{5,6},{6,7},{7,8},{8,9},{9,10},{10,1... | collective-permute-start | bytes 393224 | tf_op jit(solution)/shard_map/while/body/eval_jaxpr/ppermute | solution.py:15
  282.3 7.1 collective-permute-start.1
  289.9 14.4 %collective-permute-done.1 = f32[2,256,128]{2,1,0:T(8,128)S(1)} collective-permute-done((f32[2,256,128]{2,1,0:T(8,128)S(1)}, f32[2,256,128]{2,1,0:T(8,128)S(1)}, u32[]{:S(2)}, u32[]{:S(2)}) %collective-permute-start.1) | collective-permute-done | bytes 262176 | tf_op jit(solution)/shard_map/while/body/eval_jaxpr/ppermute | solution.py:20
  310.1 10.8 %collective-permute-done = bf16[2,256,128]{2,1,0:T(8,128)(2,1)S(1)} collective-permute-done((bf16[2,256,128]{2,1,0:T(8,128)(2,1)S(1)}, bf16[2,256,128]{2,1,0:T(8,128)(2,1)S(1)}, u32[]{:S(2)}, u32[]{:S(2)}) %collective-permute-start) | collective-permute-done | bytes 131104 | tf_op jit(solution)/shard_map/while/body/eval_jaxpr/ppermute | solution.py:15
  320.9 9.6 %collective-permute-done.1 = f32[2,256,128]{2,1,0:T(8,128)S(1)} collective-permute-done((f32[2,256,128]{2,1,0:T(8,128)S(1)}, f32[2,256,128]{2,1,0:T(8,128)S(1)}, u32[]{:S(2)}, u32[]{:S(2)}) %collective-permute-start.1) | collective-permute-done | bytes 262176 | tf_op jit(solution)/shard_map/while/body/eval_jaxpr/ppermute | solution.py:20
  335.1 10.9 %collective-permute-done = bf16[2,256,128]{2,1,0:T(8,128)(2,1)S(1)} collective-permute-done((bf16[2,256,128]{2,1,0:T(8,128)(2,1)S(1)}, bf16[2,256,128]{2,1,0:T(8,128)(2,1)S(1)}, u32[]{:S(2)}, u32[]{:S(2)}) %collective-permute-start) | collective-permute-done | bytes 131104 | tf_op jit(solution)/shard_map/while/body/eval_jaxpr/ppermute | solution.py:15
  346.0 9.4 %collective-permute-done.1 = f32[2,256,128]{2,1,0:T(8,128)S(1)} collective-permute-done((f32[2,256,128]{2,1,0:T(8,128)S(1)}, f32[2,256,128]{2,1,0:T(8,128)S(1)}, u32[]{:S(2)}, u32[]{:S(2)}) %collective-permute-start.1) | collective-permute-done | bytes 262176 | tf_op jit(solution)/shard_map/while/body/eval_jaxpr/ppermute | solution.py:20
  360.0 9.8 %collective-permute-done = bf16[2,256,128]{2,1,0:T(8,128)(2,1)S(1)} collective-permute-done((bf16[2,256,128]{2,1,0:T(8,128)(2,1)S(1)}, bf16[2,256,128]{2,1,0:T(8,128)(2,1)S(1)}, u32[]{:S(2)}, u32[]{:S(2)}) %collective-permute-start) | collective-permute-done | bytes 131104 | tf_op jit(solution)/shard_map/while/body/eval_jaxpr/ppermute | solution.py:15
  369.8 11.0 %collective-permute-done.1 = f32[2,256,128]{2,1,0:T(8,128)S(1)} collective-permute-done((f32[2,256,128]{2,1,0:T(8,128)S(1)}, f32[2,256,128]{2,1,0:T(8,128)S(1)}, u32[]{:S(2)}, u32[]{:S(2)}) %collective-permute-start.1) | collective-permute-done | bytes 262176 | tf_op jit(solution)/shard_map/while/body/eval_jaxpr/ppermute | solution.py:20
  385.4 13.7 %collective-permute-done = bf16[2,256,128]{2,1,0:T(8,128)(2,1)S(1)} collective-permute-done((bf16[2,256,128]{2,1,0:T(8,128)(2,1)S(1)}, bf16[2,256,128]{2,1,0:T(8,128)(2,1)S(1)}, u32[]{:S(2)}, u32[]{:S(2)}) %collective-permute-start) | collective-permute-done | bytes 131104 | tf_op jit(solution)/shard_map/while/body/eval_jaxpr/ppermute | solution.py:15
  399.1 7.5 collective-permute-done.1
  411.2 9.7 %collective-permute-done = bf16[2,256,128]{2,1,0:T(8,128)(2,1)S(1)} collective-permute-done((bf16[2,256,128]{2,1,0:T(8,128)(2,1)S(1)}, bf16[2,256,128]{2,1,0:T(8,128)(2,1)S(1)}, u32[]{:S(2)}, u32[]{:S(2)}) %collective-permute-start) | collective-permute-done | bytes 131104 | tf_op jit(solution)/shard_map/while/body/eval_jaxpr/ppermute | solution.py:15
  420.9 10.6 %collective-permute-done.1 = f32[2,256,128]{2,1,0:T(8,128)S(1)} collective-permute-done((f32[2,256,128]{2,1,0:T(8,128)S(1)}, f32[2,256,128]{2,1,0:T(8,128)S(1)}, u32[]{:S(2)}, u32[]{:S(2)}) %collective-permute-start.1) | collective-permute-done | bytes 262176 | tf_op jit(solution)/shard_map/while/body/eval_jaxpr/ppermute | solution.py:20
  436.1 13.3 %collective-permute-done = bf16[2,256,128]{2,1,0:T(8,128)(2,1)S(1)} collective-permute-done((bf16[2,256,128]{2,1,0:T(8,128)(2,1)S(1)}, bf16[2,256,128]{2,1,0:T(8,128)(2,1)S(1)}, u32[]{:S(2)}, u32[]{:S(2)}) %collective-permute-start) | collective-permute-done | bytes 131104 | tf_op jit(solution)/shard_map/while/body/eval_jaxpr/ppermute | solution.py:15
  449.3 9.6 %collective-permute-done.1 = f32[2,256,128]{2,1,0:T(8,128)S(1)} collective-permute-done((f32[2,256,128]{2,1,0:T(8,128)S(1)}, f32[2,256,128]{2,1,0:T(8,128)S(1)}, u32[]{:S(2)}, u32[]{:S(2)}) %collective-permute-start.1) | collective-permute-done | bytes 262176 | tf_op jit(solution)/shard_map/while/body/eval_jaxpr/ppermute | solution.py:20
  463.6 14.9 %collective-permute-done = bf16[2,256,128]{2,1,0:T(8,128)(2,1)S(1)} collective-permute-done((bf16[2,256,128]{2,1,0:T(8,128)(2,1)S(1)}, bf16[2,256,128]{2,1,0:T(8,128)(2,1)S(1)}, u32[]{:S(2)}, u32[]{:S(2)}) %collective-permute-start) | collective-permute-done | bytes 131104 | tf_op jit(solution)/shard_map/while/body/eval_jaxpr/ppermute | solution.py:15
  478.4 6.0 collective-permute-done.1
  489.0 12.6 %collective-permute-done = bf16[2,256,128]{2,1,0:T(8,128)(2,1)S(1)} collective-permute-done((bf16[2,256,128]{2,1,0:T(8,128)(2,1)S(1)}, bf16[2,256,128]{2,1,0:T(8,128)(2,1)S(1)}, u32[]{:S(2)}, u32[]{:S(2)}) %collective-permute-start) | collective-permute-done | bytes 131104 | tf_op jit(solution)/shard_map/while/body/eval_jaxpr/ppermute | solution.py:15
  501.6 5.7 collective-permute-done.1
  513.2 9.2 %collective-permute-done = bf16[2,256,128]{2,1,0:T(8,128)(2,1)S(1)} collective-permute-done((bf16[2,256,128]{2,1,0:T(8,128)(2,1)S(1)}, bf16[2,256,128]{2,1,0:T(8,128)(2,1)S(1)}, u32[]{:S(2)}, u32[]{:S(2)}) %collective-permute-start) | collective-permute-done | bytes 131104 | tf_op jit(solution)/shard_map/while/body/eval_jaxpr/ppermute | solution.py:15
  522.4 6.1 collective-permute-done.1
  534.5 7.2 collective-permute-done
  541.6 7.5 collective-permute-done.1
  553.7 8.2 collective-permute-done
  561.9 7.3 collective-permute-done.1
  573.9 8.0 collective-permute-done
  591.3 8.0 collective-permute-done
  599.3 6.1 collective-permute-done.1
  610.0 8.3 collective-permute-done
  630.2 9.2 %collective-permute-done = bf16[2,256,128]{2,1,0:T(8,128)(2,1)S(1)} collective-permute-done((bf16[2,256,128]{2,1,0:T(8,128)(2,1)S(1)}, bf16[2,256,128]{2,1,0:T(8,128)(2,1)S(1)}, u32[]{:S(2)}, u32[]{:S(2)}) %collective-permute-start) | collective-permute-done | bytes 131104 | tf_op jit(solution)/shard_map/while/body/eval_jaxpr/ppermute | solution.py:15
  648.1 5.3 collective-permute-start.1
  654.0 5.7 collective-permute-done
  659.7 9.8 %collective-permute-done.1 = f32[2,256,128]{2,1,0:T(8,128)S(1)} collective-permute-done((f32[2,256,128]{2,1,0:T(8,128)S(1)}, f32[2,256,128]{2,1,0:T(8,128)S(1)}, u32[]{:S(2)}, u32[]{:S(2)}) %collective-permute-start.1) | collective-permute-done | bytes 262176 | tf_op jit(solution)/shard_map/while/body/eval_jaxpr/ppermute | solution.py:20
  683.9 10.0 %collective-permute-done.1 = f32[2,256,128]{2,1,0:T(8,128)S(1)} collective-permute-done((f32[2,256,128]{2,1,0:T(8,128)S(1)}, f32[2,256,128]{2,1,0:T(8,128)S(1)}, u32[]{:S(2)}, u32[]{:S(2)}) %collective-permute-start.1) | collective-permute-done | bytes 262176 | tf_op jit(solution)/shard_map/while/body/eval_jaxpr/ppermute | solution.py:20
  703.6 6.4 collective-permute-done
  710.0 6.1 collective-permute-done.1
  721.3 5.2 collective-permute-start.1
  728.8 7.0 collective-permute-done.1
  735.8 5.0 collective-permute-start
  749.2 5.9 collective-permute-done.1
  762.1 8.4 collective-permute-done
  778.5 14.4 %collective-permute-done.2 = bf16[2,256,128]{2,1,0:T(8,128)(2,1)S(1)} collective-permute-done((bf16[2,256,128]{2,1,0:T(8,128)(2,1)S(1)}, bf16[2,256,128]{2,1,0:T(8,128)(2,1)S(1)}, u32[]{:S(2)}, u32[]{:S(2)}) %collective-permute-start.2) | collective-permute-done | bytes 131104 | tf_op jit(solution)/shard_map/ppermute | solution.py:20
  793.5 55.5 %all-to-all-start.7 = ((bf16[8,32,128]{2,1,0:T(8,128)(2,1)}), bf16[8,32,128]{2,1,0:T(8,128)(2,1)S(1)}, u32[]{:S(2)}, u32[]{:S(2)}) async-start(bf16[8,32,128]{2,1,0:T(8,128)(2,1)} %bitcast.41), calls=%async_computation.7 | async-start | bytes 131072 | tf_op jit(solution)/shard_map/all_to_all | solution.py:138
  868.8 8.7 all-to-all-done.6
  (602 shorter events, 301.5 us)
Async XLA Ops:
  31.9 14.3 %all-to-all-start.2 = ((bf16[32,8,640]{2,0,1:T(8,128)(2,1)}), bf16[32,8,640]{2,0,1:T(8,128)(2,1)S(1)}, u32[]{:S(2)}, u32[]{:S(2)}) async-start(bf16[32,8,640]{2,0,1:T(8,128)(2,1)} %bitcast.253), calls=%async_computation.2 | async-start | bytes 655360 | tf_op jit(solution)/shard_map/all_to_all | solution.py:37
  46.3 14.5 %all-to-all-start.4 = ((bf16[32,8,640]{2,0,1:T(8,128)(2,1)}), bf16[32,8,640]{2,0,1:T(8,128)(2,1)S(1)}, u32[]{:S(2)}, u32[]{:S(2)}) async-start(bf16[32,8,640]{2,0,1:T(8,128)(2,1)} %bitcast.252), calls=%async_computation.4 | async-start | bytes 655360 | tf_op jit(solution)/shard_map/all_to_all | solution.py:46
  60.8 15.2 %all-to-all-start.5 = ((bf16[32,8,640]{2,0,1:T(8,128)(2,1)}), bf16[32,8,640]{2,0,1:T(8,128)(2,1)}, u32[]{:S(2)}, u32[]{:S(2)}) async-start(bf16[32,8,640]{2,0,1:T(8,128)(2,1)} %bitcast.251), calls=%async_computation.5 | async-start | bytes 655360 | tf_op jit(solution)/shard_map/all_to_all | solution.py:50
  77.8 17.8 %collective-permute-start = (bf16[2,256,128]{2,1,0:T(8,128)(2,1)S(1)}, bf16[2,256,128]{2,1,0:T(8,128)(2,1)S(1)}, u32[]{:S(2)}, u32[]{:S(2)}) collective-permute-start(bf16[2,256,128]{2,1,0:T(8,128)(2,1)S(1)} %copy.135), channel_id=1, source_target_pairs={{0,1},{1,2},{2,3},{3,4},{4,5},{5,6},{6,7},{7,8},{8,9},{9,10},{10,1... | collective-permute-start | bytes 393224 | tf_op jit(solution)/shard_map/while/body/eval_jaxpr/ppermute | solution.py:15
  86.1 15.3 %collective-permute-start.1 = (f32[2,256,128]{2,1,0:T(8,128)S(1)}, f32[2,256,128]{2,1,0:T(8,128)S(1)}, u32[]{:S(2)}, u32[]{:S(2)}) collective-permute-start(f32[2,256,128]{2,1,0:T(8,128)S(1)} %maximum_add_fusion.3), channel_id=1, source_target_pairs={{0,1},{1,2},{2,3},{3,4},{4,5},{5,6},{6,7},{7,8},{8,9},{9,10},{10,1... | collective-permute-start | bytes 786440 | tf_op jit(solution)/shard_map/while/body/eval_jaxpr/ppermute | solution.py:20
  101.4 13.2 %collective-permute-start = (bf16[2,256,128]{2,1,0:T(8,128)(2,1)S(1)}, bf16[2,256,128]{2,1,0:T(8,128)(2,1)S(1)}, u32[]{:S(2)}, u32[]{:S(2)}) collective-permute-start(bf16[2,256,128]{2,1,0:T(8,128)(2,1)S(1)} %copy.135), channel_id=1, source_target_pairs={{0,1},{1,2},{2,3},{3,4},{4,5},{5,6},{6,7},{7,8},{8,9},{9,10},{10,1... | collective-permute-start | bytes 393224 | tf_op jit(solution)/shard_map/while/body/eval_jaxpr/ppermute | solution.py:15
  105.4 17.1 %collective-permute-start.1 = (f32[2,256,128]{2,1,0:T(8,128)S(1)}, f32[2,256,128]{2,1,0:T(8,128)S(1)}, u32[]{:S(2)}, u32[]{:S(2)}) collective-permute-start(f32[2,256,128]{2,1,0:T(8,128)S(1)} %maximum_add_fusion.3), channel_id=1, source_target_pairs={{0,1},{1,2},{2,3},{3,4},{4,5},{5,6},{6,7},{7,8},{8,9},{9,10},{10,1... | collective-permute-start | bytes 786440 | tf_op jit(solution)/shard_map/while/body/eval_jaxpr/ppermute | solution.py:20
  122.5 12.6 %collective-permute-start = (bf16[2,256,128]{2,1,0:T(8,128)(2,1)S(1)}, bf16[2,256,128]{2,1,0:T(8,128)(2,1)S(1)}, u32[]{:S(2)}, u32[]{:S(2)}) collective-permute-start(bf16[2,256,128]{2,1,0:T(8,128)(2,1)S(1)} %copy.135), channel_id=1, source_target_pairs={{0,1},{1,2},{2,3},{3,4},{4,5},{5,6},{6,7},{7,8},{8,9},{9,10},{10,1... | collective-permute-start | bytes 393224 | tf_op jit(solution)/shard_map/while/body/eval_jaxpr/ppermute | solution.py:15
  126.4 14.4 %collective-permute-start.1 = (f32[2,256,128]{2,1,0:T(8,128)S(1)}, f32[2,256,128]{2,1,0:T(8,128)S(1)}, u32[]{:S(2)}, u32[]{:S(2)}) collective-permute-start(f32[2,256,128]{2,1,0:T(8,128)S(1)} %maximum_add_fusion.3), channel_id=1, source_target_pairs={{0,1},{1,2},{2,3},{3,4},{4,5},{5,6},{6,7},{7,8},{8,9},{9,10},{10,1... | collective-permute-start | bytes 786440 | tf_op jit(solution)/shard_map/while/body/eval_jaxpr/ppermute | solution.py:20
  140.8 16.7 %collective-permute-start = (bf16[2,256,128]{2,1,0:T(8,128)(2,1)S(1)}, bf16[2,256,128]{2,1,0:T(8,128)(2,1)S(1)}, u32[]{:S(2)}, u32[]{:S(2)}) collective-permute-start(bf16[2,256,128]{2,1,0:T(8,128)(2,1)S(1)} %copy.135), channel_id=1, source_target_pairs={{0,1},{1,2},{2,3},{3,4},{4,5},{5,6},{6,7},{7,8},{8,9},{9,10},{10,1... | collective-permute-start | bytes 393224 | tf_op jit(solution)/shard_map/while/body/eval_jaxpr/ppermute | solution.py:15
  145.7 14.8 %collective-permute-start.1 = (f32[2,256,128]{2,1,0:T(8,128)S(1)}, f32[2,256,128]{2,1,0:T(8,128)S(1)}, u32[]{:S(2)}, u32[]{:S(2)}) collective-permute-start(f32[2,256,128]{2,1,0:T(8,128)S(1)} %maximum_add_fusion.3), channel_id=1, source_target_pairs={{0,1},{1,2},{2,3},{3,4},{4,5},{5,6},{6,7},{7,8},{8,9},{9,10},{10,1... | collective-permute-start | bytes 786440 | tf_op jit(solution)/shard_map/while/body/eval_jaxpr/ppermute | solution.py:20
  160.5 16.8 %collective-permute-start = (bf16[2,256,128]{2,1,0:T(8,128)(2,1)S(1)}, bf16[2,256,128]{2,1,0:T(8,128)(2,1)S(1)}, u32[]{:S(2)}, u32[]{:S(2)}) collective-permute-start(bf16[2,256,128]{2,1,0:T(8,128)(2,1)S(1)} %copy.135), channel_id=1, source_target_pairs={{0,1},{1,2},{2,3},{3,4},{4,5},{5,6},{6,7},{7,8},{8,9},{9,10},{10,1... | collective-permute-start | bytes 393224 | tf_op jit(solution)/shard_map/while/body/eval_jaxpr/ppermute | solution.py:15
  167.6 13.3 %collective-permute-start.1 = (f32[2,256,128]{2,1,0:T(8,128)S(1)}, f32[2,256,128]{2,1,0:T(8,128)S(1)}, u32[]{:S(2)}, u32[]{:S(2)}) collective-permute-start(f32[2,256,128]{2,1,0:T(8,128)S(1)} %maximum_add_fusion.3), channel_id=1, source_target_pairs={{0,1},{1,2},{2,3},{3,4},{4,5},{5,6},{6,7},{7,8},{8,9},{9,10},{10,1... | collective-permute-start | bytes 786440 | tf_op jit(solution)/shard_map/while/body/eval_jaxpr/ppermute | solution.py:20
  180.9 17.8 %collective-permute-start = (bf16[2,256,128]{2,1,0:T(8,128)(2,1)S(1)}, bf16[2,256,128]{2,1,0:T(8,128)(2,1)S(1)}, u32[]{:S(2)}, u32[]{:S(2)}) collective-permute-start(bf16[2,256,128]{2,1,0:T(8,128)(2,1)S(1)} %copy.135), channel_id=1, source_target_pairs={{0,1},{1,2},{2,3},{3,4},{4,5},{5,6},{6,7},{7,8},{8,9},{9,10},{10,1... | collective-permute-start | bytes 393224 | tf_op jit(solution)/shard_map/while/body/eval_jaxpr/ppermute | solution.py:15
  187.9 15.0 %collective-permute-start.1 = (f32[2,256,128]{2,1,0:T(8,128)S(1)}, f32[2,256,128]{2,1,0:T(8,128)S(1)}, u32[]{:S(2)}, u32[]{:S(2)}) collective-permute-start(f32[2,256,128]{2,1,0:T(8,128)S(1)} %maximum_add_fusion.3), channel_id=1, source_target_pairs={{0,1},{1,2},{2,3},{3,4},{4,5},{5,6},{6,7},{7,8},{8,9},{9,10},{10,1... | collective-permute-start | bytes 786440 | tf_op jit(solution)/shard_map/while/body/eval_jaxpr/ppermute | solution.py:20
  202.9 18.2 %collective-permute-start = (bf16[2,256,128]{2,1,0:T(8,128)(2,1)S(1)}, bf16[2,256,128]{2,1,0:T(8,128)(2,1)S(1)}, u32[]{:S(2)}, u32[]{:S(2)}) collective-permute-start(bf16[2,256,128]{2,1,0:T(8,128)(2,1)S(1)} %copy.135), channel_id=1, source_target_pairs={{0,1},{1,2},{2,3},{3,4},{4,5},{5,6},{6,7},{7,8},{8,9},{9,10},{10,1... | collective-permute-start | bytes 393224 | tf_op jit(solution)/shard_map/while/body/eval_jaxpr/ppermute | solution.py:15
  206.9 17.7 %collective-permute-start.1 = (f32[2,256,128]{2,1,0:T(8,128)S(1)}, f32[2,256,128]{2,1,0:T(8,128)S(1)}, u32[]{:S(2)}, u32[]{:S(2)}) collective-permute-start(f32[2,256,128]{2,1,0:T(8,128)S(1)} %maximum_add_fusion.3), channel_id=1, source_target_pairs={{0,1},{1,2},{2,3},{3,4},{4,5},{5,6},{6,7},{7,8},{8,9},{9,10},{10,1... | collective-permute-start | bytes 786440 | tf_op jit(solution)/shard_map/while/body/eval_jaxpr/ppermute | solution.py:20
  224.6 18.2 %collective-permute-start = (bf16[2,256,128]{2,1,0:T(8,128)(2,1)S(1)}, bf16[2,256,128]{2,1,0:T(8,128)(2,1)S(1)}, u32[]{:S(2)}, u32[]{:S(2)}) collective-permute-start(bf16[2,256,128]{2,1,0:T(8,128)(2,1)S(1)} %copy.135), channel_id=1, source_target_pairs={{0,1},{1,2},{2,3},{3,4},{4,5},{5,6},{6,7},{7,8},{8,9},{9,10},{10,1... | collective-permute-start | bytes 393224 | tf_op jit(solution)/shard_map/while/body/eval_jaxpr/ppermute | solution.py:15
  228.6 19.2 %collective-permute-start.1 = (f32[2,256,128]{2,1,0:T(8,128)S(1)}, f32[2,256,128]{2,1,0:T(8,128)S(1)}, u32[]{:S(2)}, u32[]{:S(2)}) collective-permute-start(f32[2,256,128]{2,1,0:T(8,128)S(1)} %maximum_add_fusion.3), channel_id=1, source_target_pairs={{0,1},{1,2},{2,3},{3,4},{4,5},{5,6},{6,7},{7,8},{8,9},{9,10},{10,1... | collective-permute-start | bytes 786440 | tf_op jit(solution)/shard_map/while/body/eval_jaxpr/ppermute | solution.py:20
  247.7 18.0 %collective-permute-start = (bf16[2,256,128]{2,1,0:T(8,128)(2,1)S(1)}, bf16[2,256,128]{2,1,0:T(8,128)(2,1)S(1)}, u32[]{:S(2)}, u32[]{:S(2)}) collective-permute-start(bf16[2,256,128]{2,1,0:T(8,128)(2,1)S(1)} %copy.135), channel_id=1, source_target_pairs={{0,1},{1,2},{2,3},{3,4},{4,5},{5,6},{6,7},{7,8},{8,9},{9,10},{10,1... | collective-permute-start | bytes 393224 | tf_op jit(solution)/shard_map/while/body/eval_jaxpr/ppermute | solution.py:15
  251.7 19.6 %collective-permute-start.1 = (f32[2,256,128]{2,1,0:T(8,128)S(1)}, f32[2,256,128]{2,1,0:T(8,128)S(1)}, u32[]{:S(2)}, u32[]{:S(2)}) collective-permute-start(f32[2,256,128]{2,1,0:T(8,128)S(1)} %maximum_add_fusion.3), channel_id=1, source_target_pairs={{0,1},{1,2},{2,3},{3,4},{4,5},{5,6},{6,7},{7,8},{8,9},{9,10},{10,1... | collective-permute-start | bytes 786440 | tf_op jit(solution)/shard_map/while/body/eval_jaxpr/ppermute | solution.py:20
  271.3 18.6 %collective-permute-start = (bf16[2,256,128]{2,1,0:T(8,128)(2,1)S(1)}, bf16[2,256,128]{2,1,0:T(8,128)(2,1)S(1)}, u32[]{:S(2)}, u32[]{:S(2)}) collective-permute-start(bf16[2,256,128]{2,1,0:T(8,128)(2,1)S(1)} %copy.135), channel_id=1, source_target_pairs={{0,1},{1,2},{2,3},{3,4},{4,5},{5,6},{6,7},{7,8},{8,9},{9,10},{10,1... | collective-permute-start | bytes 393224 | tf_op jit(solution)/shard_map/while/body/eval_jaxpr/ppermute | solution.py:15
  282.3 22.0 %collective-permute-start.1 = (f32[2,256,128]{2,1,0:T(8,128)S(1)}, f32[2,256,128]{2,1,0:T(8,128)S(1)}, u32[]{:S(2)}, u32[]{:S(2)}) collective-permute-start(f32[2,256,128]{2,1,0:T(8,128)S(1)} %maximum_add_fusion.3), channel_id=1, source_target_pairs={{0,1},{1,2},{2,3},{3,4},{4,5},{5,6},{6,7},{7,8},{8,9},{9,10},{10,1... | collective-permute-start | bytes 786440 | tf_op jit(solution)/shard_map/while/body/eval_jaxpr/ppermute | solution.py:20
  304.3 16.6 %collective-permute-start = (bf16[2,256,128]{2,1,0:T(8,128)(2,1)S(1)}, bf16[2,256,128]{2,1,0:T(8,128)(2,1)S(1)}, u32[]{:S(2)}, u32[]{:S(2)}) collective-permute-start(bf16[2,256,128]{2,1,0:T(8,128)(2,1)S(1)} %copy.135), channel_id=1, source_target_pairs={{0,1},{1,2},{2,3},{3,4},{4,5},{5,6},{6,7},{7,8},{8,9},{9,10},{10,1... | collective-permute-start | bytes 393224 | tf_op jit(solution)/shard_map/while/body/eval_jaxpr/ppermute | solution.py:15
  308.2 22.3 %collective-permute-start.1 = (f32[2,256,128]{2,1,0:T(8,128)S(1)}, f32[2,256,128]{2,1,0:T(8,128)S(1)}, u32[]{:S(2)}, u32[]{:S(2)}) collective-permute-start(f32[2,256,128]{2,1,0:T(8,128)S(1)} %maximum_add_fusion.3), channel_id=1, source_target_pairs={{0,1},{1,2},{2,3},{3,4},{4,5},{5,6},{6,7},{7,8},{8,9},{9,10},{10,1... | collective-permute-start | bytes 786440 | tf_op jit(solution)/shard_map/while/body/eval_jaxpr/ppermute | solution.py:20
  330.5 15.5 %collective-permute-start = (bf16[2,256,128]{2,1,0:T(8,128)(2,1)S(1)}, bf16[2,256,128]{2,1,0:T(8,128)(2,1)S(1)}, u32[]{:S(2)}, u32[]{:S(2)}) collective-permute-start(bf16[2,256,128]{2,1,0:T(8,128)(2,1)S(1)} %copy.135), channel_id=1, source_target_pairs={{0,1},{1,2},{2,3},{3,4},{4,5},{5,6},{6,7},{7,8},{8,9},{9,10},{10,1... | collective-permute-start | bytes 393224 | tf_op jit(solution)/shard_map/while/body/eval_jaxpr/ppermute | solution.py:15
  334.5 20.9 %collective-permute-start.1 = (f32[2,256,128]{2,1,0:T(8,128)S(1)}, f32[2,256,128]{2,1,0:T(8,128)S(1)}, u32[]{:S(2)}, u32[]{:S(2)}) collective-permute-start(f32[2,256,128]{2,1,0:T(8,128)S(1)} %maximum_add_fusion.3), channel_id=1, source_target_pairs={{0,1},{1,2},{2,3},{3,4},{4,5},{5,6},{6,7},{7,8},{8,9},{9,10},{10,1... | collective-permute-start | bytes 786440 | tf_op jit(solution)/shard_map/while/body/eval_jaxpr/ppermute | solution.py:20
  355.4 14.4 %collective-permute-start = (bf16[2,256,128]{2,1,0:T(8,128)(2,1)S(1)}, bf16[2,256,128]{2,1,0:T(8,128)(2,1)S(1)}, u32[]{:S(2)}, u32[]{:S(2)}) collective-permute-start(bf16[2,256,128]{2,1,0:T(8,128)(2,1)S(1)} %copy.135), channel_id=1, source_target_pairs={{0,1},{1,2},{2,3},{3,4},{4,5},{5,6},{6,7},{7,8},{8,9},{9,10},{10,1... | collective-permute-start | bytes 393224 | tf_op jit(solution)/shard_map/while/body/eval_jaxpr/ppermute | solution.py:15
  359.3 21.5 %collective-permute-start.1 = (f32[2,256,128]{2,1,0:T(8,128)S(1)}, f32[2,256,128]{2,1,0:T(8,128)S(1)}, u32[]{:S(2)}, u32[]{:S(2)}) collective-permute-start(f32[2,256,128]{2,1,0:T(8,128)S(1)} %maximum_add_fusion.3), channel_id=1, source_target_pairs={{0,1},{1,2},{2,3},{3,4},{4,5},{5,6},{6,7},{7,8},{8,9},{9,10},{10,1... | collective-permute-start | bytes 786440 | tf_op jit(solution)/shard_map/while/body/eval_jaxpr/ppermute | solution.py:20
  380.8 18.3 %collective-permute-start = (bf16[2,256,128]{2,1,0:T(8,128)(2,1)S(1)}, bf16[2,256,128]{2,1,0:T(8,128)(2,1)S(1)}, u32[]{:S(2)}, u32[]{:S(2)}) collective-permute-start(bf16[2,256,128]{2,1,0:T(8,128)(2,1)S(1)} %copy.135), channel_id=1, source_target_pairs={{0,1},{1,2},{2,3},{3,4},{4,5},{5,6},{6,7},{7,8},{8,9},{9,10},{10,1... | collective-permute-start | bytes 393224 | tf_op jit(solution)/shard_map/while/body/eval_jaxpr/ppermute | solution.py:15
  384.8 21.8 %collective-permute-start.1 = (f32[2,256,128]{2,1,0:T(8,128)S(1)}, f32[2,256,128]{2,1,0:T(8,128)S(1)}, u32[]{:S(2)}, u32[]{:S(2)}) collective-permute-start(f32[2,256,128]{2,1,0:T(8,128)S(1)} %maximum_add_fusion.3), channel_id=1, source_target_pairs={{0,1},{1,2},{2,3},{3,4},{4,5},{5,6},{6,7},{7,8},{8,9},{9,10},{10,1... | collective-permute-start | bytes 786440 | tf_op jit(solution)/shard_map/while/body/eval_jaxpr/ppermute | solution.py:20
  406.6 14.3 %collective-permute-start = (bf16[2,256,128]{2,1,0:T(8,128)(2,1)S(1)}, bf16[2,256,128]{2,1,0:T(8,128)(2,1)S(1)}, u32[]{:S(2)}, u32[]{:S(2)}) collective-permute-start(bf16[2,256,128]{2,1,0:T(8,128)(2,1)S(1)} %copy.135), channel_id=1, source_target_pairs={{0,1},{1,2},{2,3},{3,4},{4,5},{5,6},{6,7},{7,8},{8,9},{9,10},{10,1... | collective-permute-start | bytes 393224 | tf_op jit(solution)/shard_map/while/body/eval_jaxpr/ppermute | solution.py:15
  410.5 20.9 %collective-permute-start.1 = (f32[2,256,128]{2,1,0:T(8,128)S(1)}, f32[2,256,128]{2,1,0:T(8,128)S(1)}, u32[]{:S(2)}, u32[]{:S(2)}) collective-permute-start(f32[2,256,128]{2,1,0:T(8,128)S(1)} %maximum_add_fusion.3), channel_id=1, source_target_pairs={{0,1},{1,2},{2,3},{3,4},{4,5},{5,6},{6,7},{7,8},{8,9},{9,10},{10,1... | collective-permute-start | bytes 786440 | tf_op jit(solution)/shard_map/while/body/eval_jaxpr/ppermute | solution.py:20
  431.5 17.9 %collective-permute-start = (bf16[2,256,128]{2,1,0:T(8,128)(2,1)S(1)}, bf16[2,256,128]{2,1,0:T(8,128)(2,1)S(1)}, u32[]{:S(2)}, u32[]{:S(2)}) collective-permute-start(bf16[2,256,128]{2,1,0:T(8,128)(2,1)S(1)} %copy.135), channel_id=1, source_target_pairs={{0,1},{1,2},{2,3},{3,4},{4,5},{5,6},{6,7},{7,8},{8,9},{9,10},{10,1... | collective-permute-start | bytes 393224 | tf_op jit(solution)/shard_map/while/body/eval_jaxpr/ppermute | solution.py:15
  435.4 23.5 %collective-permute-start.1 = (f32[2,256,128]{2,1,0:T(8,128)S(1)}, f32[2,256,128]{2,1,0:T(8,128)S(1)}, u32[]{:S(2)}, u32[]{:S(2)}) collective-permute-start(f32[2,256,128]{2,1,0:T(8,128)S(1)} %maximum_add_fusion.3), channel_id=1, source_target_pairs={{0,1},{1,2},{2,3},{3,4},{4,5},{5,6},{6,7},{7,8},{8,9},{9,10},{10,1... | collective-permute-start | bytes 786440 | tf_op jit(solution)/shard_map/while/body/eval_jaxpr/ppermute | solution.py:20
  458.9 19.5 %collective-permute-start = (bf16[2,256,128]{2,1,0:T(8,128)(2,1)S(1)}, bf16[2,256,128]{2,1,0:T(8,128)(2,1)S(1)}, u32[]{:S(2)}, u32[]{:S(2)}) collective-permute-start(bf16[2,256,128]{2,1,0:T(8,128)(2,1)S(1)} %copy.135), channel_id=1, source_target_pairs={{0,1},{1,2},{2,3},{3,4},{4,5},{5,6},{6,7},{7,8},{8,9},{9,10},{10,1... | collective-permute-start | bytes 393224 | tf_op jit(solution)/shard_map/while/body/eval_jaxpr/ppermute | solution.py:15
  462.9 21.5 %collective-permute-start.1 = (f32[2,256,128]{2,1,0:T(8,128)S(1)}, f32[2,256,128]{2,1,0:T(8,128)S(1)}, u32[]{:S(2)}, u32[]{:S(2)}) collective-permute-start(f32[2,256,128]{2,1,0:T(8,128)S(1)} %maximum_add_fusion.3), channel_id=1, source_target_pairs={{0,1},{1,2},{2,3},{3,4},{4,5},{5,6},{6,7},{7,8},{8,9},{9,10},{10,1... | collective-permute-start | bytes 786440 | tf_op jit(solution)/shard_map/while/body/eval_jaxpr/ppermute | solution.py:20
  484.4 17.2 %collective-permute-start = (bf16[2,256,128]{2,1,0:T(8,128)(2,1)S(1)}, bf16[2,256,128]{2,1,0:T(8,128)(2,1)S(1)}, u32[]{:S(2)}, u32[]{:S(2)}) collective-permute-start(bf16[2,256,128]{2,1,0:T(8,128)(2,1)S(1)} %copy.135), channel_id=1, source_target_pairs={{0,1},{1,2},{2,3},{3,4},{4,5},{5,6},{6,7},{7,8},{8,9},{9,10},{10,1... | collective-permute-start | bytes 393224 | tf_op jit(solution)/shard_map/while/body/eval_jaxpr/ppermute | solution.py:15
  488.4 18.9 %collective-permute-start.1 = (f32[2,256,128]{2,1,0:T(8,128)S(1)}, f32[2,256,128]{2,1,0:T(8,128)S(1)}, u32[]{:S(2)}, u32[]{:S(2)}) collective-permute-start(f32[2,256,128]{2,1,0:T(8,128)S(1)} %maximum_add_fusion.3), channel_id=1, source_target_pairs={{0,1},{1,2},{2,3},{3,4},{4,5},{5,6},{6,7},{7,8},{8,9},{9,10},{10,1... | collective-permute-start | bytes 786440 | tf_op jit(solution)/shard_map/while/body/eval_jaxpr/ppermute | solution.py:20
  507.3 15.0 %collective-permute-start = (bf16[2,256,128]{2,1,0:T(8,128)(2,1)S(1)}, bf16[2,256,128]{2,1,0:T(8,128)(2,1)S(1)}, u32[]{:S(2)}, u32[]{:S(2)}) collective-permute-start(bf16[2,256,128]{2,1,0:T(8,128)(2,1)S(1)} %copy.135), channel_id=1, source_target_pairs={{0,1},{1,2},{2,3},{3,4},{4,5},{5,6},{6,7},{7,8},{8,9},{9,10},{10,1... | collective-permute-start | bytes 393224 | tf_op jit(solution)/shard_map/while/body/eval_jaxpr/ppermute | solution.py:15
  511.3 17.2 %collective-permute-start.1 = (f32[2,256,128]{2,1,0:T(8,128)S(1)}, f32[2,256,128]{2,1,0:T(8,128)S(1)}, u32[]{:S(2)}, u32[]{:S(2)}) collective-permute-start(f32[2,256,128]{2,1,0:T(8,128)S(1)} %maximum_add_fusion.3), channel_id=1, source_target_pairs={{0,1},{1,2},{2,3},{3,4},{4,5},{5,6},{6,7},{7,8},{8,9},{9,10},{10,1... | collective-permute-start | bytes 786440 | tf_op jit(solution)/shard_map/while/body/eval_jaxpr/ppermute | solution.py:20
  528.5 13.1 %collective-permute-start = (bf16[2,256,128]{2,1,0:T(8,128)(2,1)S(1)}, bf16[2,256,128]{2,1,0:T(8,128)(2,1)S(1)}, u32[]{:S(2)}, u32[]{:S(2)}) collective-permute-start(bf16[2,256,128]{2,1,0:T(8,128)(2,1)S(1)} %copy.135), channel_id=1, source_target_pairs={{0,1},{1,2},{2,3},{3,4},{4,5},{5,6},{6,7},{7,8},{8,9},{9,10},{10,1... | collective-permute-start | bytes 393224 | tf_op jit(solution)/shard_map/while/body/eval_jaxpr/ppermute | solution.py:15
  532.5 16.6 %collective-permute-start.1 = (f32[2,256,128]{2,1,0:T(8,128)S(1)}, f32[2,256,128]{2,1,0:T(8,128)S(1)}, u32[]{:S(2)}, u32[]{:S(2)}) collective-permute-start(f32[2,256,128]{2,1,0:T(8,128)S(1)} %maximum_add_fusion.3), channel_id=1, source_target_pairs={{0,1},{1,2},{2,3},{3,4},{4,5},{5,6},{6,7},{7,8},{8,9},{9,10},{10,1... | collective-permute-start | bytes 786440 | tf_op jit(solution)/shard_map/while/body/eval_jaxpr/ppermute | solution.py:20
  549.1 12.8 %collective-permute-start = (bf16[2,256,128]{2,1,0:T(8,128)(2,1)S(1)}, bf16[2,256,128]{2,1,0:T(8,128)(2,1)S(1)}, u32[]{:S(2)}, u32[]{:S(2)}) collective-permute-start(bf16[2,256,128]{2,1,0:T(8,128)(2,1)S(1)} %copy.135), channel_id=1, source_target_pairs={{0,1},{1,2},{2,3},{3,4},{4,5},{5,6},{6,7},{7,8},{8,9},{9,10},{10,1... | collective-permute-start | bytes 393224 | tf_op jit(solution)/shard_map/while/body/eval_jaxpr/ppermute | solution.py:15
  553.1 16.2 %collective-permute-start.1 = (f32[2,256,128]{2,1,0:T(8,128)S(1)}, f32[2,256,128]{2,1,0:T(8,128)S(1)}, u32[]{:S(2)}, u32[]{:S(2)}) collective-permute-start(f32[2,256,128]{2,1,0:T(8,128)S(1)} %maximum_add_fusion.3), channel_id=1, source_target_pairs={{0,1},{1,2},{2,3},{3,4},{4,5},{5,6},{6,7},{7,8},{8,9},{9,10},{10,1... | collective-permute-start | bytes 786440 | tf_op jit(solution)/shard_map/while/body/eval_jaxpr/ppermute | solution.py:20
  573.2 13.4 %collective-permute-start.1 = (f32[2,256,128]{2,1,0:T(8,128)S(1)}, f32[2,256,128]{2,1,0:T(8,128)S(1)}, u32[]{:S(2)}, u32[]{:S(2)}) collective-permute-start(f32[2,256,128]{2,1,0:T(8,128)S(1)} %maximum_add_fusion.3), channel_id=1, source_target_pairs={{0,1},{1,2},{2,3},{3,4},{4,5},{5,6},{6,7},{7,8},{8,9},{9,10},{10,1... | collective-permute-start | bytes 786440 | tf_op jit(solution)/shard_map/while/body/eval_jaxpr/ppermute | solution.py:20
  590.6 14.8 %collective-permute-start.1 = (f32[2,256,128]{2,1,0:T(8,128)S(1)}, f32[2,256,128]{2,1,0:T(8,128)S(1)}, u32[]{:S(2)}, u32[]{:S(2)}) collective-permute-start(f32[2,256,128]{2,1,0:T(8,128)S(1)} %maximum_add_fusion.3), channel_id=1, source_target_pairs={{0,1},{1,2},{2,3},{3,4},{4,5},{5,6},{6,7},{7,8},{8,9},{9,10},{10,1... | collective-permute-start | bytes 786440 | tf_op jit(solution)/shard_map/while/body/eval_jaxpr/ppermute | solution.py:20
  605.4 13.0 %collective-permute-start = (bf16[2,256,128]{2,1,0:T(8,128)(2,1)S(1)}, bf16[2,256,128]{2,1,0:T(8,128)(2,1)S(1)}, u32[]{:S(2)}, u32[]{:S(2)}) collective-permute-start(bf16[2,256,128]{2,1,0:T(8,128)(2,1)S(1)} %copy.135), channel_id=1, source_target_pairs={{0,1},{1,2},{2,3},{3,4},{4,5},{5,6},{6,7},{7,8},{8,9},{9,10},{10,1... | collective-permute-start | bytes 393224 | tf_op jit(solution)/shard_map/while/body/eval_jaxpr/ppermute | solution.py:15
  609.4 13.6 %collective-permute-start.1 = (f32[2,256,128]{2,1,0:T(8,128)S(1)}, f32[2,256,128]{2,1,0:T(8,128)S(1)}, u32[]{:S(2)}, u32[]{:S(2)}) collective-permute-start(f32[2,256,128]{2,1,0:T(8,128)S(1)} %maximum_add_fusion.3), channel_id=1, source_target_pairs={{0,1},{1,2},{2,3},{3,4},{4,5},{5,6},{6,7},{7,8},{8,9},{9,10},{10,1... | collective-permute-start | bytes 786440 | tf_op jit(solution)/shard_map/while/body/eval_jaxpr/ppermute | solution.py:20
  623.0 16.5 %collective-permute-start = (bf16[2,256,128]{2,1,0:T(8,128)(2,1)S(1)}, bf16[2,256,128]{2,1,0:T(8,128)(2,1)S(1)}, u32[]{:S(2)}, u32[]{:S(2)}) collective-permute-start(bf16[2,256,128]{2,1,0:T(8,128)(2,1)S(1)} %copy.135), channel_id=1, source_target_pairs={{0,1},{1,2},{2,3},{3,4},{4,5},{5,6},{6,7},{7,8},{8,9},{9,10},{10,1... | collective-permute-start | bytes 393224 | tf_op jit(solution)/shard_map/while/body/eval_jaxpr/ppermute | solution.py:15
  628.2 15.9 %collective-permute-start.1 = (f32[2,256,128]{2,1,0:T(8,128)S(1)}, f32[2,256,128]{2,1,0:T(8,128)S(1)}, u32[]{:S(2)}, u32[]{:S(2)}) collective-permute-start(f32[2,256,128]{2,1,0:T(8,128)S(1)} %maximum_add_fusion.3), channel_id=1, source_target_pairs={{0,1},{1,2},{2,3},{3,4},{4,5},{5,6},{6,7},{7,8},{8,9},{9,10},{10,1... | collective-permute-start | bytes 786440 | tf_op jit(solution)/shard_map/while/body/eval_jaxpr/ppermute | solution.py:20
  644.1 15.6 %collective-permute-start = (bf16[2,256,128]{2,1,0:T(8,128)(2,1)S(1)}, bf16[2,256,128]{2,1,0:T(8,128)(2,1)S(1)}, u32[]{:S(2)}, u32[]{:S(2)}) collective-permute-start(bf16[2,256,128]{2,1,0:T(8,128)(2,1)S(1)} %copy.135), channel_id=1, source_target_pairs={{0,1},{1,2},{2,3},{3,4},{4,5},{5,6},{6,7},{7,8},{8,9},{9,10},{10,1... | collective-permute-start | bytes 393224 | tf_op jit(solution)/shard_map/while/body/eval_jaxpr/ppermute | solution.py:15
  648.1 21.3 %collective-permute-start.1 = (f32[2,256,128]{2,1,0:T(8,128)S(1)}, f32[2,256,128]{2,1,0:T(8,128)S(1)}, u32[]{:S(2)}, u32[]{:S(2)}) collective-permute-start(f32[2,256,128]{2,1,0:T(8,128)S(1)} %maximum_add_fusion.3), channel_id=1, source_target_pairs={{0,1},{1,2},{2,3},{3,4},{4,5},{5,6},{6,7},{7,8},{8,9},{9,10},{10,1... | collective-permute-start | bytes 786440 | tf_op jit(solution)/shard_map/while/body/eval_jaxpr/ppermute | solution.py:20
  669.5 14.4 %collective-permute-start = (bf16[2,256,128]{2,1,0:T(8,128)(2,1)S(1)}, bf16[2,256,128]{2,1,0:T(8,128)(2,1)S(1)}, u32[]{:S(2)}, u32[]{:S(2)}) collective-permute-start(bf16[2,256,128]{2,1,0:T(8,128)(2,1)S(1)} %copy.135), channel_id=1, source_target_pairs={{0,1},{1,2},{2,3},{3,4},{4,5},{5,6},{6,7},{7,8},{8,9},{9,10},{10,1... | collective-permute-start | bytes 393224 | tf_op jit(solution)/shard_map/while/body/eval_jaxpr/ppermute | solution.py:15
  674.9 19.0 %collective-permute-start.1 = (f32[2,256,128]{2,1,0:T(8,128)S(1)}, f32[2,256,128]{2,1,0:T(8,128)S(1)}, u32[]{:S(2)}, u32[]{:S(2)}) collective-permute-start(f32[2,256,128]{2,1,0:T(8,128)S(1)} %maximum_add_fusion.3), channel_id=1, source_target_pairs={{0,1},{1,2},{2,3},{3,4},{4,5},{5,6},{6,7},{7,8},{8,9},{9,10},{10,1... | collective-permute-start | bytes 786440 | tf_op jit(solution)/shard_map/while/body/eval_jaxpr/ppermute | solution.py:20
  693.9 16.2 %collective-permute-start = (bf16[2,256,128]{2,1,0:T(8,128)(2,1)S(1)}, bf16[2,256,128]{2,1,0:T(8,128)(2,1)S(1)}, u32[]{:S(2)}, u32[]{:S(2)}) collective-permute-start(bf16[2,256,128]{2,1,0:T(8,128)(2,1)S(1)} %copy.135), channel_id=1, source_target_pairs={{0,1},{1,2},{2,3},{3,4},{4,5},{5,6},{6,7},{7,8},{8,9},{9,10},{10,1... | collective-permute-start | bytes 393224 | tf_op jit(solution)/shard_map/while/body/eval_jaxpr/ppermute | solution.py:15
  699.5 16.7 %collective-permute-start.1 = (f32[2,256,128]{2,1,0:T(8,128)S(1)}, f32[2,256,128]{2,1,0:T(8,128)S(1)}, u32[]{:S(2)}, u32[]{:S(2)}) collective-permute-start(f32[2,256,128]{2,1,0:T(8,128)S(1)} %maximum_add_fusion.3), channel_id=1, source_target_pairs={{0,1},{1,2},{2,3},{3,4},{4,5},{5,6},{6,7},{7,8},{8,9},{9,10},{10,1... | collective-permute-start | bytes 786440 | tf_op jit(solution)/shard_map/while/body/eval_jaxpr/ppermute | solution.py:20
  721.3 14.5 %collective-permute-start.1 = (f32[2,256,128]{2,1,0:T(8,128)S(1)}, f32[2,256,128]{2,1,0:T(8,128)S(1)}, u32[]{:S(2)}, u32[]{:S(2)}) collective-permute-start(f32[2,256,128]{2,1,0:T(8,128)S(1)} %maximum_add_fusion.3), channel_id=1, source_target_pairs={{0,1},{1,2},{2,3},{3,4},{4,5},{5,6},{6,7},{7,8},{8,9},{9,10},{10,1... | collective-permute-start | bytes 786440 | tf_op jit(solution)/shard_map/while/body/eval_jaxpr/ppermute | solution.py:20
  735.8 13.4 %collective-permute-start = (bf16[2,256,128]{2,1,0:T(8,128)(2,1)S(1)}, bf16[2,256,128]{2,1,0:T(8,128)(2,1)S(1)}, u32[]{:S(2)}, u32[]{:S(2)}) collective-permute-start(bf16[2,256,128]{2,1,0:T(8,128)(2,1)S(1)} %copy.135), channel_id=1, source_target_pairs={{0,1},{1,2},{2,3},{3,4},{4,5},{5,6},{6,7},{7,8},{8,9},{9,10},{10,1... | collective-permute-start | bytes 393224 | tf_op jit(solution)/shard_map/while/body/eval_jaxpr/ppermute | solution.py:15
  755.1 15.3 %collective-permute-start = (bf16[2,256,128]{2,1,0:T(8,128)(2,1)S(1)}, bf16[2,256,128]{2,1,0:T(8,128)(2,1)S(1)}, u32[]{:S(2)}, u32[]{:S(2)}) collective-permute-start(bf16[2,256,128]{2,1,0:T(8,128)(2,1)S(1)} %copy.135), channel_id=1, source_target_pairs={{0,1},{1,2},{2,3},{3,4},{4,5},{5,6},{6,7},{7,8},{8,9},{9,10},{10,1... | collective-permute-start | bytes 393224 | tf_op jit(solution)/shard_map/while/body/eval_jaxpr/ppermute | solution.py:15
  759.7 15.4 %collective-permute-start.1 = (f32[2,256,128]{2,1,0:T(8,128)S(1)}, f32[2,256,128]{2,1,0:T(8,128)S(1)}, u32[]{:S(2)}, u32[]{:S(2)}) collective-permute-start(f32[2,256,128]{2,1,0:T(8,128)S(1)} %maximum_add_fusion.3), channel_id=1, source_target_pairs={{0,1},{1,2},{2,3},{3,4},{4,5},{5,6},{6,7},{7,8},{8,9},{9,10},{10,1... | collective-permute-start | bytes 786440 | tf_op jit(solution)/shard_map/while/body/eval_jaxpr/ppermute | solution.py:20
  778.4 14.5 %collective-permute-start.2 = (bf16[2,256,128]{2,1,0:T(8,128)(2,1)S(1)}, bf16[2,256,128]{2,1,0:T(8,128)(2,1)S(1)}, u32[]{:S(2)}, u32[]{:S(2)}) collective-permute-start(bf16[2,256,128]{2,1,0:T(8,128)(2,1)S(1)} %fusion.42), channel_id=1, source_target_pairs={{0,1},{1,2},{2,3},{3,4},{4,5},{5,6},{6,7},{7,8},{8,9},{9,10},{10,1... | collective-permute-start | bytes 393224 | tf_op jit(solution)/shard_map/ppermute | solution.py:20
  793.5 60.6 %all-to-all-start.7 = ((bf16[8,32,128]{2,1,0:T(8,128)(2,1)}), bf16[8,32,128]{2,1,0:T(8,128)(2,1)S(1)}, u32[]{:S(2)}, u32[]{:S(2)}) async-start(bf16[8,32,128]{2,1,0:T(8,128)(2,1)} %bitcast.41), calls=%async_computation.7 | async-start | bytes 131072 | tf_op jit(solution)/shard_map/all_to_all | solution.py:138
  863.3 14.2 %all-to-all-start.6 = ((bf16[8,32,640]{2,1,0:T(8,128)(2,1)}), bf16[8,32,640]{2,1,0:T(8,128)(2,1)S(1)}, u32[]{:S(2)}, u32[]{:S(2)}) async-start(bf16[8,32,640]{2,1,0:T(8,128)(2,1)} %convert_element_type.162), calls=%async_computation.6 | async-start | bytes 655360 | tf_op jit(solution)/shard_map/all_to_all | solution.py:137
  (13 other events, 177.3 us)
where the time goes:
time: 887 us; the launch traced here: 878 us
  waiting for transfers between devices  525 us (59%)
  starting transfers between devices  251 us (28%)
  matrix products  62.8 us (7%)
  local copies, waits for them, and re-layouts  23 us (3%)
  other arithmetic  11.9 us (1%)
    ppermute x31, waiting for transfers between devices, passed_along(): return lax.ppermute(array, axis, pairs)  245 us
    ppermute x32, waiting for transfers between devices, shifted(): lax.ppermute(array, axis, [(i, (i + by) % size) for i in range(size)])  227 us
    ppermute x31, starting transfers between devices, passed_along(): return lax.ppermute(array, axis, pairs)  87 us
    ppermute x32, starting transfers between devices, shifted(): lax.ppermute(array, axis, [(i, (i + by) % size) for i in range(size)])  71.9 us
    all_to_all x1, starting transfers between devices, local(): lax.all_to_all(key_low, 'head', split_axis=0, concat_axis=1, tiled=True)  55.5 us
  transfers between devices with their start and end apart: 72, of which 71 were waited for; matrix products, arithmetic and copies ran while one was open for 10% of the time, Pallas kernels for 0%

commit v1 on v0

v1 whole, which is shorter than its diff:
```python
import jax
import jax.numpy as jnp
from jax import lax
from jax.experimental import pallas as pl
from jax.experimental.pallas import tpu as pltpu
from jax.sharding import PartitionSpec as P

QH = 40
KVH = 8
HD = 128
BLOCK = 128
GS = QH // KVH
TOK = 32
GW = GS * HD
PIECE = 64
ROWS = GS * PIECE
NX = 4
NZ = 8
PEERS = 8
LISTW = 32
SCALE = HD ** -0.5
LOG2E = 1.4426950408889634
MESH = pl.DeviceIdType.MESH
F32 = jnp.float32
BF16 = jnp.bfloat16
NT = (((1,), (1,)), ((), ()))
NN = (((1,), (0,)), ((), ()))


def coords():
    blk = lax.axis_index("blk")
    head = lax.axis_index("head")
    y = blk // 8
    x = (blk // 2) % 4
    z = (blk % 2) * 4 + head // 2
    return y, x, z, head % 2


def device(y, x, z, core):
    return {"blk": (y * 4 + x) * 2 + z // 4, "head": (z % 4) * 2 + core}


def remote(src, dst, send_sem, recv_sem, device_id):
    return pltpu.make_async_remote_copy(
        src_ref=src,
        dst_ref=dst,
        send_sem=send_sem,
        recv_sem=recv_sem,
        device_id=device_id,
        device_id_type=MESH,
    )


def signal_group(bar, y, x, z, core, me):
    for d in range(1, PEERS):
        p = (me + d) % PEERS
        pl.semaphore_signal(bar, inc=1, device_id=device(y, p // 2, z, p % 2), device_id_type=MESH)
    for step in (1, NZ - 1):
        pl.semaphore_signal(
            bar, inc=1, device_id=device(y, x, (z + step) % NZ, core), device_id_type=MESH
        )
    cross = (y == 1) | (y == 2)

    @pl.when(cross)
    def _():
        pl.semaphore_signal(bar, inc=1, device_id=device(3 - y, x, z, core), device_id_type=MESH)

    pl.semaphore_wait(bar, PEERS - 1 + 2 + cross.astype(jnp.int32))


CHAINS = ((0, 0, 4), (0, 1, 3), (1, 1, 4), (1, 0, 3))


def gather_kernel(
    q, k, v, o, do, lse, lists,
    qg, dog, stg, lsg, kvg,
    stat_src, list_src,
    kv_s, kv_r, kv_l, big_s, big_r, big_l, st_s, st_r, st_l, ls_s, ls_r, ls_l,
    ring_s, ring_r, cr_s, cr_r, crst_s, crst_r, crls_s, crls_r,
):
    y, x, z, core = coords()
    me = x * 2 + core
    bar = pltpu.get_barrier_semaphore()
    signal_group(bar, y, x, z, core, me)

    def cols(ref, g, width):
        return ref.at[:, pl.ds(pl.multiple_of(g * width, 128), width)]

    def kv_slot(s, piece, zz):
        return kvg.at[zz, piece, s // 2, pl.ds((s % 2) * TOK, TOK), :]

    def kv_copy(d, piece):
        p = (me + d) % PEERS
        src = (k, v)[piece]
        return remote(
            cols(src, p, HD), kv_slot(me, piece, z),
            kv_s.at[piece, p], kv_r.at[piece, me], device(y, p // 2, z, p % 2),
        )

    def kv_recv(d, piece):
        s = (me + PEERS - d) % PEERS
        src = (k, v)[piece]
        return remote(
            cols(src, s, HD), kv_slot(s, piece, z),
            kv_s.at[piece, s], kv_r.at[piece, s], device(y, s // 2, z, s % 2),
        )

    def big_copy(d, which):
        p = (me + d) % PEERS
        src, dst = ((q, qg), (do, dog))[which]
        return remote(
            cols(src, p, GW), dst.at[0, me],
            big_s.at[which, p], big_r.at[which, me], device(y, p // 2, z, p % 2),
        )

    def big_recv(s, which):
        src, dst = ((q, qg), (do, dog))[which]
        return remote(
            cols(src, s, GW), dst.at[0, s],
            big_s.at[which, s], big_r.at[which, s], device(y, s // 2, z, s % 2),
        )

    def st_copy(d):
        p = (me + d) % PEERS
        return remote(
            stat_src.at[p], stg.at[0, me], st_s.at[p], st_r.at[me], device(y, p // 2, z, p % 2)
        )

    def st_recv(d):
        s = (me + PEERS - d) % PEERS
        return remote(
            stat_src.at[s], stg.at[0, s], st_s.at[s], st_r.at[s], device(y, s // 2, z, s % 2)
        )

    def ls_copy(d):
        xx = (x + d) % NX
        return remote(list_src, lsg.at[0, x], ls_s.at[xx], ls_r.at[x], device(y, xx, z, core))

    def ls_recv(d):
        xx = (x + NX - d) % NX
        return remote(list_src, lsg.at[0, xx], ls_s.at[xx], ls_r.at[xx], device(y, xx, z, core))

    order = (2, 3, 4, 5, 6, 7, 1)
    for piece in (0, 1):
        for d in order:
            kv_copy(d, piece).start()
    kv_local = [
        pltpu.make_async_copy(cols((k, v)[piece], me, HD), kv_slot(me, piece, z), kv_l.at[piece])
        for piece in (0, 1)
    ]
    big_local = [
        pltpu.make_async_copy(cols(q, me, GW), qg.at[0, me], big_l.at[0]),
        pltpu.make_async_copy(cols(do, me, GW), dog.at[0, me], big_l.at[1]),
    ]
    for c in kv_local + big_local:
        c.start()
    for d in order:
        for which in (0, 1):
            big_copy(d, which).start()

    rows = lists[...]
    count = jnp.sum(jnp.where(rows >= 0, 1.0, 0.0), axis=1, keepdims=True).astype(jnp.int32)
    early = jnp.sum(
        jnp.where((rows >= 0) & (rows < 32), 1.0, 0.0), axis=1, keepdims=True
    ).astype(jnp.int32)
    list_src[...] = jnp.zeros((8, 128), jnp.int32)
    list_src[0:2, 0:LISTW] = rows
    lane = lax.broadcasted_iota(jnp.int32, (2, 128), 1)
    list_src[4:6, :] = jnp.where(lane == 0, count, early)
    for d in range(1, NX):
        ls_copy(d).start()
    ls_local = pltpu.make_async_copy(list_src, lsg.at[0, x], ls_l)
    ls_local.start()

    lane = lax.broadcasted_iota(jnp.int32, (TOK, 128), 1)
    for g in range(KVH):
        block = jnp.zeros((TOK, 128), F32)
        for r in range(GS):
            h = g * GS + r
            own = slice(h * HD, (h + 1) * HD)
            delta = jnp.sum(do[:, own].astype(F32) * o[:, own].astype(F32), axis=1, keepdims=True)
            block = jnp.where(lane == r, lse[:, h : h + 1] * LOG2E, block)
            block = jnp.where(lane == 8 + r, delta, block)
        stat_src[g] = block
    for d in order:
        st_copy(d).start()
    st_local = pltpu.make_async_copy(stat_src.at[me], stg.at[0, me], st_l)
    st_local.start()

    def ring_copy(direction, piece, step):
        sign = (1, NZ - 1)[direction]
        back = (NZ - 1, 1)[direction]
        chunk = (z + back * step) % NZ
        part = kvg.at[chunk, piece]
        return remote(
            part, part, ring_s.at[direction, piece, step], ring_r.at[direction, piece, step],
            device(y, x, (z + sign) % NZ, core),
        )

    def ring_recv(direction, piece, step):
        back = (NZ - 1, 1)[direction]
        chunk = (z + back * (step + 1)) % NZ
        part = kvg.at[chunk, piece]
        return remote(
            part, part, ring_s.at[direction, piece, step], ring_r.at[direction, piece, step],
            device(y, x, (z + back) % NZ, core),
        )

    for piece in (0, 1):
        for d in range(1, PEERS):
            kv_recv(d, piece).wait_recv()
        kv_local[piece].wait()
        for direction in (0, 1):
            ring_copy(direction, piece, 0).start()

    def cross_copy(s, which):
        ref = (qg, dog)[which]
        return remote(
            ref.at[0, s], ref.at[1, s], cr_s.at[which, s], cr_r.at[which, s],
            device(3 - y, x, z, core),
        )

    for c in big_local:
        c.wait()

    @pl.when(y == 2)
    def _():
        for which in (0, 1):
            cross_copy(me, which).start()

    def forward(ds):
        for d in ds:
            s = (me + PEERS - d) % PEERS
            for which in (0, 1):
                big_recv(s, which).wait_recv()

            @pl.when(y == 2)
            def _():
                for which in (0, 1):
                    cross_copy(s, which).start()

    groups = ((7, 1), (2, 3), (4, 5, 6), ())
    for step in range(4):
        for direction, piece, steps in CHAINS:
            if step < steps:
                ring_recv(direction, piece, step).wait_recv()
                if step + 1 < steps:
                    ring_copy(direction, piece, step + 1).start()
        forward(groups[step])

    for d in range(1, PEERS):
        st_recv(d).wait_recv()
    for d in range(1, NX):
        ls_recv(d).wait_recv()
    st_local.wait()
    ls_local.wait()

    crst = remote(stg.at[0], stg.at[1], crst_s, crst_r, device(3 - y, x, z, core))
    crls = remote(lsg.at[0], lsg.at[1], crls_s, crls_r, device(3 - y, x, z, core))

    @pl.when(y == 2)
    def _():
        crst.start()
        crls.start()

    for d in range(1, PEERS):
        for i in (0, 1):
            kv_copy(d, i).wait_send()
            big_copy(d, i).wait_send()
        st_copy(d).wait_send()
    for d in range(1, NX):
        ls_copy(d).wait_send()
    for direction, piece, steps in CHAINS:
        for step in range(steps):
            ring_copy(direction, piece, step).wait_send()

    @pl.when(y == 2)
    def _():
        for s in range(PEERS):
            for which in (0, 1):
                cross_copy(s, which).wait_send()
        crst.wait_send()
        crls.wait_send()

    @pl.when(y == 1)
    def _():
        for s in range(PEERS):
            for which in (0, 1):
                cross_copy(s, which).wait_recv()
        crst.wait_recv()
        crls.wait_recv()


def gather(q, k, v, o, do, lse, lists):
    vmem = pl.BlockSpec(memory_space=pltpu.VMEM)
    dma = pltpu.SemaphoreType.DMA
    return pl.pallas_call(
        gather_kernel,
        out_shape=(
            jax.ShapeDtypeStruct((2, PEERS, TOK, GW), BF16),
            jax.ShapeDtypeStruct((2, PEERS, TOK, GW), BF16),
            jax.ShapeDtypeStruct((2, PEERS, TOK, 128), F32),
            jax.ShapeDtypeStruct((2, NX, 8, 128), jnp.int32),
            jax.ShapeDtypeStruct((NZ, 2, NX, PIECE, HD), BF16),
        ),
        in_specs=[vmem] * 7,
        out_specs=(vmem,) * 5,
        scratch_shapes=[
            pltpu.VMEM((KVH, TOK, 128), F32),
            pltpu.VMEM((8, 128), jnp.int32),
            dma((2, PEERS)), dma((2, PEERS)), dma((2,)),
            dma((2, PEERS)), dma((2, PEERS)), dma((2,)),
            dma((PEERS,)), dma((PEERS,)), dma,
            dma((NX,)), dma((NX,)), dma,
            dma((2, 2, 4)), dma((2, 2, 4)),
            dma((2, PEERS)), dma((2, PEERS)),
            dma, dma, dma, dma,
        ],
        compiler_params=pltpu.CompilerParams(collective_id=0, has_side_effects=True),
        name="gather",
    )(q, k, v, o, do, lse, lists)


def attend_kernel(
    lists, qg, dog, stg, kvg, dq, dkv,
    qs, dos, qt, dot, lseb, delb, dqa, dka, dva,
):
    y, x, z, core = coords()
    half = (z % 4) // 2
    base = y * 16
    for ref in (dka, dva):
        ref[...] = jnp.zeros_like(ref)
    r_id = lax.broadcasted_iota(jnp.int32, (128, 128), 0)
    c_id = lax.broadcasted_iota(jnp.int32, (128, 128), 1)
    eye = jnp.where(r_id == c_id, 1.0, 0.0).astype(BF16)
    row_tok = (z % 2) * PIECE + lax.broadcasted_iota(jnp.int32, (ROWS, 128), 0) % PIECE
    key_tok = lax.broadcasted_iota(jnp.int32, (ROWS, 128), 1)

    def chunk(i, carry):
        part = i // NX
        xx = i % NX
        total = lists[part, xx, 4 + half, 0]
        early = lists[part, xx, 4 + half, 1]
        own = part == 0
        lo = jnp.where(own & (y == 2), early, 0)
        hi = jnp.where(own, total, jnp.where(y == 1, early, 0))
        n = hi - lo
        diag = jnp.where(own, xx * 4 + z // 2, -1)

        @pl.when(n > 0)
        def _():
            for c in range(2):
                st = stg[part, xx * 2 + c]
                for r in range(GS):
                    at = slice(r * PIECE + c * TOK, r * PIECE + (c + 1) * TOK)
                    col = slice(r * HD, (r + 1) * HD)
                    qs[at, :] = qg[part, xx * 2 + c, :, col]
                    dos[at, :] = dog[part, xx * 2 + c, :, col]
                    lseb[at, :] = jnp.broadcast_to(st[:, r : r + 1], (TOK, 128))
                    delb[at, :] = jnp.broadcast_to(st[:, 8 + r : 9 + r], (TOK, 128))
            qt[...] = lax.dot_general(eye, qs[...], NT, preferred_element_type=F32).astype(BF16)
            dot[...] = lax.dot_general(eye, dos[...], NT, preferred_element_type=F32).astype(BF16)
            dqa[...] = jnp.zeros_like(dqa)

            def block(piece, b):
                zz = (b % 4) * 2
                return jnp.concatenate(
                    [kvg[zz, piece, b // 4], kvg[zz + 1, piece, b // 4]], axis=0
                )

            def pair(j, masked):
                a = lists[part, xx, half, j] - base
                if masked:
                    has = j + 1 < hi
                    b = jnp.where(has, lists[part, xx, half, jnp.where(has, j + 1, j)] - base, a)
                else:
                    b = lists[part, xx, half, j + 1] - base
                keys = jnp.concatenate([block(0, a), block(0, b)], axis=0)
                values = jnp.concatenate([block(1, a), block(1, b)], axis=0)
                s = lax.dot_general(qs[...], keys, NT, preferred_element_type=F32)
                lse2 = jnp.concatenate([lseb[...], lseb[...]], axis=1)
                del2 = jnp.concatenate([delb[...], delb[...]], axis=1)
                p = jnp.exp2(s * (SCALE * LOG2E) - lse2)
                if masked:
                    ta = row_tok + jnp.where(a == diag, 0, BLOCK)
                    tb = row_tok + jnp.where(has, jnp.where(b == diag, 0, BLOCK), -2 * BLOCK)
                    seen = jnp.concatenate([key_tok <= ta, key_tok <= tb], axis=1)
                    p = jnp.where(seen, p, 0.0)
                dp = lax.dot_general(dos[...], values, NT, preferred_element_type=F32)
                ds = (p * (dp - del2)).astype(BF16)
                pb = p.astype(BF16)
                dvt = lax.dot_general(dot[...], pb, NN, preferred_element_type=F32)
                dkt = lax.dot_general(qt[...], ds, NN, preferred_element_type=F32)
                dqa[...] += lax.dot_general(ds, keys, NN, preferred_element_type=F32)
                dva[a] += dvt[:, :BLOCK]
                dka[a] += dkt[:, :BLOCK]
                dva[b] += dvt[:, BLOCK:]
                dka[b] += dkt[:, BLOCK:]

            full = (n - 1) // 2

            def step(t, carry):
                pair(lo + 2 * t, False)
                return carry

            lax.fori_loop(0, full, step, 0)
            pair(lo + 2 * full, True)
            for c in range(2):
                for r in range(GS):
                    at = slice(r * PIECE + c * TOK, r * PIECE + (c + 1) * TOK)
                    col = slice(r * HD, (r + 1) * HD)
                    dq[part, xx * 2 + c, :, col] = (dqa[at, :] * SCALE).astype(BF16)

        @pl.when((n <= 0) & (y == 1))
        def _():
            for c in range(2):
                dq[part, xx * 2 + c] = jnp.zeros((TOK, GW), BF16)

        return carry

    lax.fori_loop(0, jnp.where(y == 1, 2 * NX, NX), chunk, 0)

    def finish(b, carry):
        zz = (b % 4) * 2
        for piece, ref, scale in ((0, dka, SCALE), (1, dva, 1.0)):
            low = (ref[b] * scale).astype(BF16)
            out = lax.dot_general(eye, low, NT, preferred_element_type=F32).astype(BF16)
            dkv[zz, piece, b // 4] = out[:PIECE]
            dkv[zz + 1, piece, b // 4] = out[PIECE:]
        return carry

    lax.fori_loop(0, 16, finish, 0)


def attend(lists, qg, dog, stg, kvg):
    vmem = pl.BlockSpec(memory_space=pltpu.VMEM)
    return pl.pallas_call(
        attend_kernel,
        out_shape=(
            jax.ShapeDtypeStruct((2, PEERS, TOK, GW), BF16),
            jax.ShapeDtypeStruct((NZ, 2, NX, PIECE, HD), BF16),
        ),
        in_specs=[pl.BlockSpec(memory_space=pltpu.SMEM)] + [vmem] * 4,
        out_specs=(vmem, vmem),
        scratch_shapes=[
            pltpu.VMEM((ROWS, HD), BF16),
            pltpu.VMEM((ROWS, HD), BF16),
            pltpu.VMEM((HD, ROWS), BF16),
            pltpu.VMEM((HD, ROWS), BF16),
            pltpu.VMEM((ROWS, 128), F32),
            pltpu.VMEM((ROWS, 128), F32),
            pltpu.VMEM((ROWS, HD), F32),
            pltpu.VMEM((16, HD, BLOCK), F32),
            pltpu.VMEM((16, HD, BLOCK), F32),
        ],
        name="attend",
    )(lists, qg, dog, stg, kvg)


def give_kernel(
    dq, dkv, gq, gk, gv,
    land, total, acc_in, acc_out, final,
    cr_s, cr_r, ring_s, ring_r, q_s, q_r, q_l, kv_s, kv_r, kv_l,
):
    y, x, z, core = coords()
    me = x * 2 + core
    bar = pltpu.get_barrier_semaphore()
    signal_group(bar, y, x, z, core, me)

    def cols(ref, g, width):
        return ref.at[:, pl.ds(pl.multiple_of(g * width, 128), width)]

    def cross_copy(s):
        return remote(dq.at[1, s], land.at[s], cr_s.at[s], cr_r.at[s], device(3 - y, x, z, core))

    slots = [(me + d) % PEERS for d in (2, 3, 4, 5, 6, 7, 1, 0)]

    @pl.when(y == 1)
    def _():
        for s in slots:
            cross_copy(s).start()

    def ring_copy(direction, piece, steps, step):
        sign = (1, NZ - 1)[direction]
        owner = (z + sign * (steps - step)) % NZ
        if step == 0:
            src = dkv.at[owner, piece]
        else:
            src = acc_out.at[direction, piece, step]
        return remote(
            src, acc_in.at[direction, piece, step],
            ring_s.at[direction, piece, step], ring_r.at[direction, piece, step],
            device(y, x, (z + sign) % NZ, core),
        )

    for direction, piece, steps in CHAINS:
        ring_copy(direction, piece, steps, 0).start()

    def q_copy(src, p):
        return remote(
            src.at[p], cols(gq, me, GW), q_s.at[p], q_r.at[me], device(y, p // 2, z, p % 2)
        )

    def q_recv(s):
        return remote(
            total.at[s], cols(gq, s, GW), q_s.at[s], q_r.at[s], device(y, s // 2, z, s % 2)
        )

    q_local = pltpu.make_async_copy(total.at[me], cols(gq, me, GW), q_l)
    q_local_direct = pltpu.make_async_copy(dq.at[0, me], cols(gq, me, GW), q_l)

    @pl.when(y != 2)
    def _():
        for p in slots[:-1]:
            q_copy(dq.at[0], p).start()
        q_local_direct.start()

    def add_cross(some):
        @pl.when(y == 2)
        def _():
            for s in some:
                cross_copy(s).wait_recv()
                total[s] = (dq[0, s].astype(F32) + land[s].astype(F32)).astype(BF16)
                if s is slots[-1]:
                    q_local.start()
                else:
                    q_copy(total, s).start()

    groups = ((), slots[0:2], slots[2:5], slots[5:8])
    for step in range(1, 4):
        for direction, piece, steps in CHAINS:
            if step < steps:
                sign = (1, NZ - 1)[direction]
                owner = (z + sign * (steps - step)) % NZ
                ring_copy(direction, piece, steps, step - 1).wait_recv()
                acc_out[direction, piece, step] = (
                    acc_in[direction, piece, step - 1].astype(F32)
                    + dkv[owner, piece].astype(F32)
                ).astype(BF16)
                ring_copy(direction, piece, steps, step).start()
        add_cross(groups[step])

    def kv_copy(piece, p):
        return remote(
            final.at[piece, p // 2, pl.ds((p % 2) * TOK, TOK), :],
            cols((gk, gv)[piece], me, HD),
            kv_s.at[piece, p], kv_r.at[piece, me], device(y, p // 2, z, p % 2),
        )

    def kv_recv(piece, s):
        return remote(
            final.at[piece, s // 2, pl.ds((s % 2) * TOK, TOK), :],
            cols((gk, gv)[piece], s, HD),
            kv_s.at[piece, s], kv_r.at[piece, s], device(y, s // 2, z, s % 2),
        )

    kv_local = []
    for piece in (0, 1):
        last = [(d, steps) for d, pc, steps in CHAINS if pc == piece]
        for direction, steps in last:
            ring_copy(direction, piece, steps, steps - 1).wait_recv()
        (d0, s0), (d1, s1) = last
        final[piece] = (
            acc_in[d0, piece, s0 - 1].astype(F32)
            + acc_in[d1, piece, s1 - 1].astype(F32)
            + dkv[z, piece].astype(F32)
        ).astype(BF16)
        for p in slots[:-1]:
            kv_copy(piece, p).start()
        local = pltpu.make_async_copy(
            final.at[piece, x, pl.ds(core * TOK, TOK), :], cols((gk, gv)[piece], me, HD), kv_l.at[piece]
        )
        local.start()
        kv_local.append(local)

    @pl.when(y == 1)
    def _():
        for s in slots:
            cross_copy(s).wait_send()

    for direction, piece, steps in CHAINS:
        for step in range(steps):
            ring_copy(direction, piece, steps, step).wait_send()
    for p in slots[:-1]:
        q_copy(total, p).wait_send()
        q_recv(p).wait_recv()
        for piece in (0, 1):
            kv_copy(piece, p).wait_send()
            kv_recv(piece, p).wait_recv()
    q_local.wait()
    for c in kv_local:
        c.wait()


def give(dq, dkv):
    vmem = pl.BlockSpec(memory_space=pltpu.VMEM)
    dma = pltpu.SemaphoreType.DMA
    return pl.pallas_call(
        give_kernel,
        out_shape=(
            jax.ShapeDtypeStruct((TOK, QH * HD), BF16),
            jax.ShapeDtypeStruct((TOK, KVH * HD), BF16),
            jax.ShapeDtypeStruct((TOK, KVH * HD), BF16),
        ),
        in_specs=[vmem] * 2,
        out_specs=(vmem,) * 3,
        scratch_shapes=[
            pltpu.VMEM((PEERS, TOK, GW), BF16),
            pltpu.VMEM((PEERS, TOK, GW), BF16),
            pltpu.VMEM((2, 2, 4, NX, PIECE, HD), BF16),
            pltpu.VMEM((2, 2, 4, NX, PIECE, HD), BF16),
            pltpu.VMEM((2, NX, PIECE, HD), BF16),
            dma((PEERS,)), dma((PEERS,)),
            dma((2, 2, 4)), dma((2, 2, 4)),
            dma((PEERS,)), dma((PEERS,)), dma,
            dma((2, PEERS)), dma((2, PEERS)), dma((2,)),
        ],
        compiler_params=pltpu.CompilerParams(collective_id=1, has_side_effects=True),
        name="give",
    )(dq, dkv)


def local(query_act, key_act, value_act, attn_out, grad_out, log_sum, kv_lists):
    qg, dog, stg, lsg, kvg = gather(
        query_act, key_act, value_act, attn_out, grad_out, log_sum, kv_lists
    )
    dq, dkv = attend(lsg, qg, dog, stg, kvg)
    return give(dq, dkv)


def solution(mesh):
    row = P(("blk", "head"), None)
    return jax.shard_map(
        local,
        mesh=mesh,
        in_specs=(row,) * 6 + (P("blk", None),),
        out_specs=(row,) * 3,
        check_vma=False,
    )
```

time: 887 us -> 95.4 us (0.11); the launches traced: 878 us -> 95.9 us
  waiting for transfers between devices: 525 us -> 0 us
  starting transfers between devices: 251 us -> 0 us
  Pallas kernels: 0 us -> 92 us
  matrix products: 62.8 us -> 0 us
  local copies, waits for them, and re-layouts: 23 us -> 3.24 us
  other arithmetic: 11.9 us -> 0 us
    ppermute x63 -> x0, waiting for transfers between devices: 472 us -> none  [the longest x31 245 us: passed_along(): return lax.ppermute(array, axis, pairs)]
    ppermute x63 -> x0, starting transfers between devices: 159 us -> none  [the longest x31 87 us: passed_along(): return lax.ppermute(array, axis, pairs)]
    all_to_all x9 -> x0, starting transfers between devices: 92.4 us -> none  [the longest x1 55.5 us: local(): lax.all_to_all(key_low, 'head', split_axis=0, concat_axis=1, tiled=True)]
    pallas_call x0 -> x3, Pallas kernels: none -> 92 us  [the longest x1 37.5 us: gather(): pl.pallas_call(gather_kernel, out_shape=(jax.ShapeDtypeStruct((2, PEERS,...]
    dot_general x160 -> x0, matrix products: 62.8 us -> none  [the longest x32 17 us: attend(): jnp.einsum('kgts,skd->tkgd', grad_scores, key_block, preferred_element_ty...]
    all_to_all x9 -> x0, waiting for transfers between devices: 52.6 us -> none  [the longest x1 9.27 us: local(): lax.all_to_all(query_act.astype(jnp.float32), 'head', split_axis=1, conca...]
  transfers between devices with their start and end apart: 72 -> 0, of which waited for: 71 -> 0; matrix products, arithmetic and copies ran while one was open for 10% -> 0% of each run, Pallas kernels for 0% -> 0%
where the time goes in v1:
time: 95.4 us; the launch traced here: 95.9 us
  Pallas kernels  92 us (96%)
  local copies, waits for them, and re-layouts  3.24 us (3%)
    pallas_call x1, Pallas kernels, gather(): pl.pallas_call(gather_kernel, out_shape=(jax.ShapeDtypeStruct((2, PEERS,...  37.5 us
    pallas_call x1, Pallas kernels, give(): pl.pallas_call(give_kernel, out_shape=(jax.ShapeDtypeStruct((TOK, QH * HD...  30.2 us
    pallas_call x1, Pallas kernels, attend(): pl.pallas_call(attend_kernel, out_shape=(jax.ShapeDtypeStruct((2, PEERS,...  24.2 us
    unnamed x7, local copies, waits for them, and re-layouts  3.24 us

profile of v1, /device:TPU:9, one launch (start us, length us, event | category | flops | bytes accessed | tf_op | source)
XLA Modules:
  0.0 95.9 jit_solution(4582367641559881730)
XLA Ops:
  0.6 37.5 %gather.1 = (bf16[2,8,32,640]{3,2,1,0:T(8,128)(2,1)}, bf16[2,8,32,640]{3,2,1,0:T(8,128)(2,1)}, f32[2,8,32,128]{3,2,1,0:T(8,128)}, s32[2,4,8,128]{3,2,1,0:T(8,128)}, bf16[8,2,4,64,128]{4,3,2,1,0:T(8,128)(2,1)}) custom-call(bf16[32,5120]{1,0:T(8,128)(2,1)} %q.1, bf16[32,1024]{1,0:T(8,128)(2,1)} %k.1, bf16[32,1024]{1,0:T(8,128)(2,1)} %v.1, bf16[32,5120]{1,0:T(8,128)(2,1)} %o.1, ...), custom_call_target="tpu_custom_call" | custom-call | tf_op jit(solution)/shard_map/gather/pallas_call | solution.py:297
  38.2 24.2 %attend.1 = (bf16[2,8,32,640]{3,2,1,0:T(8,128)(2,1)}, bf16[8,2,4,64,128]{4,3,2,1,0:T(8,128)(2,1)}) custom-call(s32[2,4,8,128]{3,2,1,0:T(8,128)} %get-tuple-element.10.lists, bf16[2,8,32,640]{3,2,1,0:T(8,128)(2,1)} %get-tuple-element.11.qg, bf16[2,8,32,640]{3,2,1,0:T(8,128)(2,1)} %get-tuple-element.12.dog, f32[2,8,32,128]{3,2,1,0:T(8,128)} %get-tuple-element.13.stg, ...), custom_call_target="tpu_custom_call" | custom-call | tf_op jit(solution)/shard_map/attend/pallas_call | solution.py:437
  62.4 30.2 %give.1 = (bf16[32,5120]{1,0:T(8,128)(2,1)}, bf16[32,1024]{1,0:T(8,128)(2,1)}, bf16[32,1024]{1,0:T(8,128)(2,1)}) custom-call(bf16[2,8,32,640]{3,2,1,0:T(8,128)(2,1)} %get-tuple-element.15.dq, bf16[8,2,4,64,128]{4,3,2,1,0:T(8,128)(2,1)} %get-tuple-element.16.dkv), custom_call_target="tpu_custom_call" | custom-call | tf_op jit(solution)/shard_map/give/pallas_call | solution.py:598
  92.7 0.0 copy-start.1
  92.7 1.7 %copy.13 = bf16[32,5120]{1,0:T(8,128)(2,1)} copy(bf16[32,5120]{1,0:T(8,128)(2,1)} %get-tuple-element.20) | data formatting | bytes 655360
  94.4 0.0 copy-done.1
  94.4 0.0 copy-start
  94.4 0.6 copy.14
  95.1 0.2 copy-done
  95.3 0.6 copy.15
Async XLA Ops:
  92.7 1.8 %copy-start.1 = (bf16[32,1024]{1,0:T(8,128)(2,1)S(1)}, bf16[32,1024]{1,0:T(8,128)(2,1)}, u32[]{:S(2)}) copy-start(bf16[32,1024]{1,0:T(8,128)(2,1)} %get-tuple-element.21) | copy-start | bytes 196612
  94.4 0.9 copy-start
